TPU v7x, 32 devices: a whole 2x2x4 slice. The times are simulated.
32 devices in a mesh: row: 8 (over y, x, core), col: 4 (over z).
Axes of the slice: x: 2, y: 2, z: 4, core: 2. Of those that a mesh axis runs over, the one named last changes fastest.
Arguments:
- integrals: float32 [1024, 8, 8192], P(None, 'row', 'col'), may hold values from -6 to 6, as said below
- amplitudes: float32 [1024, 8, 8192], P(None, 'row', 'col'), as said below
- tile_lists: int32 [4, 3], replicated, may hold values from 0 to 3, as said below
- gap_index: int32 [8192], replicated, may hold values from 0 to 511
- pair_gaps: float32 [512], replicated, may hold values from 0.5 to 4
Outputs:
- updated: float32 [1024, 8, 8192], P(None, 'row', 'col')
Inputs may be any that keep to these rules, and one draw needn't show every extreme that they name: `integrals`: symmetric matrix. `amplitudes`: symmetric matrix. `tile_lists`: row t holds 3 distinct tile indices, among them t itself; s appears in row t exactly when t appears in row s.
All inputs are finite; a program needn't handle non-finite values.
Results may differ from a plain program's by a relative error of at most 0.0036.
Values may be sent and summed in bfloat16 or wider, within the bound.
A program may use at most 192 MiB of HBM per device.

v0:
```python
import jax
import jax.numpy as jnp
from jax import lax
from jax.sharding import PartitionSpec as P


def lookup_gaps(indices, pair_gaps):
    table_ids = jnp.arange(pair_gaps.shape[0], dtype=jnp.int32)
    return jnp.sum(
        jnp.where(indices[:, None] == table_ids[None, :], pair_gaps[None, :], 0.0), axis=1
    )


def per_device(integrals, amplitudes, tile_lists, gap_index, pair_gaps):
    rows_here = integrals.shape[0]
    block_width = integrals.shape[2]
    stride = lax.axis_size("row")
    matrix_order = rows_here * stride
    row_place = lax.axis_index("row")
    col_place = lax.axis_index("col")
    tile_count = tile_lists.shape[0]
    per_tile = block_width // stride
    my_list = lax.dynamic_slice_in_dim(tile_lists, col_place, 1, 0)[0]
    local_int = integrals[:, 0, :]
    int_low = local_int.astype(jnp.bfloat16)
    amp_tiles = amplitudes[:, 0, :].astype(jnp.bfloat16).reshape(tile_count, per_tile, block_width)
    compact = amp_tiles[my_list][:, :, None, :]
    amp_strip = lax.all_gather(compact, "row", axis=2, tiled=True)
    selector = (my_list[:, None] == jnp.arange(tile_count, dtype=jnp.int32)[None, :]).astype(
        jnp.bfloat16
    )
    amp_full = jnp.einsum("kt,kjrb->tjrb", selector, amp_strip).reshape(matrix_order, block_width)
    coupled = jnp.dot(
        lax.all_gather(int_low, "col", axis=1, tiled=True),
        amp_full,
        preferred_element_type=jnp.float32,
    )
    pieces = coupled.reshape(rows_here, block_width // stride, stride)
    arrived = lax.all_to_all(pieces, "row", split_axis=2, concat_axis=1, tiled=True)
    stacked = arrived.reshape(rows_here, stride, block_width // stride).reshape(
        matrix_order, block_width // stride
    )
    mirrored = lax.all_to_all(stacked, "col", split_axis=0, concat_axis=1, tiled=True)
    transposed = mirrored.T
    residual = local_int + coupled + transposed
    index_rows = lax.dynamic_slice_in_dim(gap_index.reshape(rows_here, stride), row_place, 1, 1)[
        :, 0
    ]
    index_cols = lax.dynamic_slice_in_dim(gap_index, col_place * block_width, block_width, 0)
    gap_rows = lookup_gaps(index_rows, pair_gaps)
    gap_cols = lookup_gaps(index_cols, pair_gaps)
    updated = -residual / (gap_rows[:, None] + gap_cols[None, :])
    return updated[:, None, :]


def solution(mesh):
    placed = (P(None, "row", "col"), P(None, "row", "col"), P(), P(), P())
    return jax.shard_map(
        per_device, mesh=mesh, in_specs=placed, out_specs=P(None, "row", "col"), check_vma=False
    )
```

profile of v0, /device:TPU:0, one launch (start us, length us, event | category | flops | bytes accessed | tf_op | source)
XLA Modules:
  0.0 829.0 jit_solution(2965992016563527453)
XLA Ops:
  6.5 0.0 all-gather.6.cloned.1.call-start
  6.5 0.7 fusion.7
  7.2 7.1 convert_element_type.11
  14.4 4.6 copy.38
  19.0 4.8 gather_fusion
  23.8 0.0 all-gather.6.cloned.1.call-update
  23.8 0.0 all-gather.4.cloned.1.call-start
  23.9 21.1 %copy.29 = f32[1024,1,2048]{0,2,1:T(8,128)} copy(f32[1024,1,2048]{2,1,0:T(1,128)} %param.5) | data formatting | bytes 16777216 | tf_op args[0]
  45.0 6.0 bitcast_convert_fusion
  51.0 0.0 all-gather.4.cloned.1.call-update
  51.0 0.7 fusion.8
  51.7 100.2 %all-gather.6.cloned.1.call-done = bf16[3,256,16384]{2,1,0:T(8,128)(2,1)} async-done(((bf16[3,256,2048]{2,1,0:T(8,128)(2,1)}), bf16[3,256,16384]{2,1,0:T(8,128)(2,1)}) %all-gather.6.cloned.1.call-update) | async-done | bytes 25165840 | tf_op jit(solution)/shard_map/all_gather | solution.py:28
  151.9 33.0 %copy.30 = bf16[3,256,16384]{1,2,0:T(8,128)(2,1)} copy(bf16[3,256,16384]{2,1,0:T(8,128)(2,1)} %all-gather.6.cloned.1.call-done) | data formatting | bytes 50331648 | tf_op jit(solution)/shard_map/all_gather | solution.py:28
  184.9 53.2 %copy.31 = bf16[3,256,8,2048]{3,0,2,1:T(4,128)(2,1)} copy(bf16[3,256,8,2048]{1,3,2,0:T(8,128)(2,1)} %bitcast.47) | data formatting | bytes 50331648 | tf_op jit(solution)/shard_map/all_gather | solution.py:28
  238.1 30.8 %fusion.4 = bf16[4,256,8,2048]{3,0,2,1:T(4,128)(2,1)} fusion(bf16[3,256,8,2048]{3,0,2,1:T(4,128)(2,1)} %copy.31, s32[3]{0:T(128)S(1)} %fusion.8), kind=kOutput, calls=%fused_computation.16 | convolution fusion | flops 100663312 | bytes 58720268 | tf_op jit(solution)/shard_map/kt,kjrb->tjrb/dot_general | solution.py:32
  268.9 30.0 %copy.32 = bf16[4,256,8,2048]{3,2,1,0:T(8,128)(2,1)} copy(bf16[4,256,8,2048]{3,0,2,1:T(4,128)(2,1)} %fusion.4) | data formatting | bytes 67108864 | tf_op jit(solution)/shard_map/kt,kjrb->tjrb/dot_general | solution.py:32
  298.9 141.4 %all-gather.4.cloned.1.call-done = bf16[1024,8192]{0,1:T(8,128)(2,1)} async-done(((bf16[1024,2048]{0,1:T(8,128)(2,1)}), bf16[1024,8192]{0,1:T(8,128)(2,1)}) %all-gather.4.cloned.1.call-update) | async-done | bytes 16777232 | tf_op jit(solution)/shard_map/all_gather | solution.py:34
  440.3 43.6 %fusion.9 = f32[2048,1024]{1,0:T(8,128)} fusion(bf16[8192,2048]{1,0:T(8,128)(2,1)} %bitcast.50, bf16[1024,8192]{0,1:T(8,128)(2,1)} %all-gather.4.cloned.1.call-done), kind=kOutput, calls=%fused_computation.21 | convolution fusion | flops 34359738368 | bytes 58720256 | tf_op jit(solution)/shard_map/dot_general | solution.py:33
  483.9 9.2 %copy.33 = f32[1024,256,8]{1,0,2:T(8,128)} copy(f32[1024,256,8]{0,2,1:T(8,128)} %bitcast.48) | data formatting | bytes 16777216 | tf_op jit(solution)/shard_map/reshape | solution.py:38
  493.1 97.8 %all_to_all.34 = f32[1024,256,8]{1,0,2:T(8,128)S(1)} all-to-all(f32[1024,256,8]{1,0,2:T(8,128)} %copy.33), channel_id=1, replica_groups=mesh['row'=8,'col'=4] {'row'}, dimensions={2} | all-to-all | bytes 16777216 | tf_op jit(solution)/shard_map/all_to_all | solution.py:39
  590.9 8.1 copy.34
  599.0 0.0 copy-start
  599.0 0.0 copy-start.1
  599.0 5.8 all-to-all-start.1
  604.7 0.0 copy-done
  604.8 0.3 reshape.52
  605.1 0.4 dynamic-slice_reduce_fusion
  605.4 0.0 copy-done.1
  605.5 0.5 select_reduce_fusion.1
  605.9 0.9 select_reduce_fusion
  606.9 180.7 %all-to-all-done.1 = f32[4,2048,256]{2,1,0:T(8,128)} async-done(((f32[4,2048,256]{2,1,0:T(8,128)}), f32[4,2048,256]{2,1,0:T(8,128)}, u32[]{:S(2)}, u32[]{:S(2)}) %all-to-all-start.1) | async-done | bytes 8388640 | tf_op jit(solution)/shard_map/all_to_all | solution.py:43
  787.5 4.4 copy.39
  792.0 9.6 %fusion.2 = f32[1024,1,2048]{0,2,1:T(8,128)} fusion(f32[2048,1024]{1,0:T(8,128)S(1)} %bitcast.49, f32[2048,1024]{1,0:T(8,128)} %fusion.9, f32[1024,1,2048]{0,2,1:T(8,128)} %copy.29, f32[2048]{0:T(1024)S(1)} %select_reduce_fusion, f32[1024]{0:T(1024)S(1)} %select_reduce_fusion.1), kind=kLoop, calls=%fused_computation.4 | loop fusion | flops 10485760 | bytes 33566720 | tf_op jit(solution)/shard_map/broadcast_in_dim | solution.py:53
  801.6 20.5 %copy.36 = f32[1024,1,2048]{2,1,0:T(1,128)} copy(f32[1024,1,2048]{0,2,1:T(8,128)} %fusion.2) | data formatting | bytes 16777216 | tf_op jit(solution)/shard_map/broadcast_in_dim | solution.py:53
  (2 shorter events, 0.0 us)
Async XLA Ops:
  6.5 145.4 %all-gather.6.cloned.1.call-start = ((), (), s32[]{:S(2)}) async-start(), calls=%async_computation.3 | async-start | bytes 28311552 | tf_op jit(solution)/shard_map/all_gather | solution.py:28
  23.8 416.4 %all-gather.4.cloned.1.call-start = ((), (), s32[]{:S(2)}) async-start(), calls=%async_computation.2 | async-start | bytes 20971520 | tf_op jit(solution)/shard_map/all_gather | solution.py:34
  599.0 5.8 copy-start
  599.0 6.5 copy-start.1
  599.0 188.6 %all-to-all-start.1 = ((f32[4,2048,256]{2,1,0:T(8,128)}), f32[4,2048,256]{2,1,0:T(8,128)}, u32[]{:S(2)}, u32[]{:S(2)}) async-start(f32[4,2048,256]{2,1,0:T(8,128)} %bitcast.51), calls=%async_computation.1 | async-start | bytes 16777216 | tf_op jit(solution)/shard_map/all_to_all | solution.py:43
Sparse Core Ops, SparseCore 0:
  24.0 127.9 all-gather.5
  153.5 286.7 all-gather.3
where the time goes:
time: 833 us; the launch traced here: 829 us
  waiting for transfers between devices  422 us (51%)
  local copies, waits for them, and re-layouts  190 us (23%)
  blocking collectives  97.8 us (12%)
  matrix products  74.4 us (9%)
  other arithmetic  24.9 us (3%)
  between operations  13.5 us (2%)
    all_to_all x1, waiting for transfers between devices, per_device(): lax.all_to_all(stacked, 'col', split_axis=0, concat_axis=1, tiled=True)  181 us
    all_gather x1, waiting for transfers between devices, per_device(): lax.all_gather(int_low, 'col', axis=1, tiled=True)  141 us
    all_gather x1, waiting for transfers between devices, per_device(): amp_strip = lax.all_gather(compact, 'row', axis=2, tiled=True)  100 us
    all_to_all x1, blocking collectives, per_device(): lax.all_to_all(pieces, 'row', split_axis=2, concat_axis=1, tiled=True)  97.8 us
    all_gather x2, local copies, waits for them, and re-layouts, per_device(): amp_strip = lax.all_gather(compact, 'row', axis=2, tiled=True)  86.2 us
    dot_general x1, matrix products, per_device(): jnp.dot(lax.all_gather(int_low, 'col', axis=1, tiled=True), amp_full, pre...  43.6 us
    dot_general x1, matrix products, per_device(): jnp.einsum('kt,kjrb->tjrb', selector, amp_strip)  30.8 us
    dot_general x1, local copies, waits for them, and re-layouts, per_device(): jnp.einsum('kt,kjrb->tjrb', selector, amp_strip)  30 us
  transfers between devices with their start and end apart: 3, of which 3 were waited for; matrix products, arithmetic and copies ran while one was open for 21% of the time, Pallas kernels for 0%

commit v1 on v0

--- a/solution.py
+++ b/solution.py
@@ -25,7 +25,25 @@
     int_low = local_int.astype(jnp.bfloat16)
     amp_tiles = amplitudes[:, 0, :].astype(jnp.bfloat16).reshape(tile_count, per_tile, block_width)
     compact = amp_tiles[my_list][:, :, None, :]
-    amp_strip = lax.all_gather(compact, "row", axis=2, tiled=True)
+    spare = lax.axis_index("row")
+    kept_arr = lax.axis_size("row")
+    right_arr, everything, tall = (kept_arr, spare, compact.shape[2])
+    trail = [(t, (t + 1) % right_arr) for t in range(right_arr)]
+    amp_strip = jnp.zeros((*compact.shape[:2], right_arr * tall, *compact.shape[3:]), compact.dtype)
+    amp_strip = lax.dynamic_update_slice_in_dim(amp_strip, compact, everything * tall, axis=2)
+    f_now = v_now = compact
+    q_next = right_arr // 2
+    buffers = [(t, (t - 1) % right_arr) for t in range(right_arr)]
+    for rr in [*range(1, q_next + 1)]:
+        f_now = lax.ppermute(f_now, "row", perm=trail)
+        amp_strip = lax.dynamic_update_slice_in_dim(
+            amp_strip, f_now, (everything - rr) % right_arr * tall, axis=2
+        )
+        if rr < right_arr - q_next:
+            v_now = lax.ppermute(v_now, axis_name="row", perm=buffers)
+            amp_strip = lax.dynamic_update_slice_in_dim(
+                amp_strip, v_now, (everything + rr) % right_arr * tall, axis=2
+            )
     selector = (my_list[:, None] == jnp.arange(tile_count, dtype=jnp.int32)[None, :]).astype(
         jnp.bfloat16
     )

time: 833 us -> 760 us (0.912)
  waiting for transfers between devices: 422 us -> 356 us
  local copies, waits for them, and re-layouts: 190 us -> 165 us
  starting transfers between devices: 5.82 us -> 15.5 us
    ppermute x0 -> x7, waiting for transfers between devices: none -> 176 us  [the longest x4 160 us: per_device(): f_now = lax.ppermute(f_now, 'row', perm=trail)]
    all_gather x1, waiting for transfers between devices: 141 us -> 0.01 us  [per_device(): lax.all_gather(int_low, 'col', axis=1, tiled=True)]
    all_gather x1 -> x0, waiting for transfers between devices: 100 us -> none  [per_device(): amp_strip = lax.all_gather(compact, 'row', axis=2, tiled=True)]
    all_gather x2 -> x0, local copies, waits for them, and re-layouts: 86.2 us -> none  [per_device(): amp_strip = lax.all_gather(compact, 'row', axis=2, tiled=True)]
    dynamic_update_slice x0 -> x8, local copies, waits for them, and re-layouts: none -> 45 us  [the longest x4 22.4 us: per_device(): lax.dynamic_update_slice_in_dim(amp_strip, f_now, (everything - rr) % rig...]
    broadcast_in_dim x0 -> x1, local copies, waits for them, and re-layouts: none -> 17.4 us  [per_device(): jnp.zeros((*compact.shape[:2], right_arr * tall, *compact.shape[3:]), com...]
    ppermute x0 -> x7, starting transfers between devices: none -> 9.67 us  [the longest x3 8.47 us: per_device(): v_now = lax.ppermute(v_now, axis_name='row', perm=buffers)]
    unnamed x6 -> x12, local copies, waits for them, and re-layouts: 25.7 us -> 25.6 us
  transfers between devices with their start and end apart: 3 -> 9, of which waited for: 3 -> 7; matrix products, arithmetic and copies ran while one was open for 21% -> 19% of each run, Pallas kernels for 0% -> 0%
where the time goes in v1:
time: 760 us; the launch traced here: 751 us
  waiting for transfers between devices  356 us (47%)
  local copies, waits for them, and re-layouts  165 us (22%)
  blocking collectives  102 us (13%)
  matrix products  74.6 us (10%)
  other arithmetic  24.2 us (3%)
  starting transfers between devices  15.5 us (2%)
  between operations  13.7 us (2%)
    all_to_all x1, waiting for transfers between devices, per_device(): lax.all_to_all(stacked, 'col', split_axis=0, concat_axis=1, tiled=True)  181 us
    ppermute x4, waiting for transfers between devices, per_device(): f_now = lax.ppermute(f_now, 'row', perm=trail)  160 us
    all_to_all x1, blocking collectives, per_device(): lax.all_to_all(pieces, 'row', split_axis=2, concat_axis=1, tiled=True)  102 us
    dot_general x1, matrix products, per_device(): jnp.dot(lax.all_gather(int_low, 'col', axis=1, tiled=True), amp_full, pre...  44 us
    dot_general x1, matrix products, per_device(): jnp.einsum('kt,kjrb->tjrb', selector, amp_strip)  30.6 us
    dot_general x1, local copies, waits for them, and re-layouts, per_device(): jnp.einsum('kt,kjrb->tjrb', selector, amp_strip)  30 us
    unnamed x12, local copies, waits for them, and re-layouts  25.6 us
    dynamic_update_slice x4, local copies, waits for them, and re-layouts, per_device(): lax.dynamic_update_slice_in_dim(amp_strip, f_now, (everything - rr) % rig...  22.4 us
  transfers between devices with their start and end apart: 9, of which 7 were waited for; matrix products, arithmetic and copies ran while one was open for 19% of the time, Pallas kernels for 0%

profile of v1, /device:TPU:0, one launch (start us, length us, event | category | flops | bytes accessed | tf_op | source)
XLA Modules:
  0.0 750.6 jit_solution(1522510357664279216)
XLA Ops:
  6.5 20.5 %copy.35 = f32[1024,1,2048]{0,2,1:T(8,128)} copy(f32[1024,1,2048]{2,1,0:T(1,128)} %param.5) | data formatting | bytes 16777216 | tf_op args[0]
  27.1 6.0 bitcast_convert_fusion
  33.1 0.0 all-gather.2.cloned.1.call-update
  33.2 7.1 convert_element_type.11
  40.3 0.0 copy-start.4
  40.3 4.8 copy.50
  45.1 0.0 copy-done.4
  45.1 3.7 gather_fusion
  48.9 0.6 collective-permute-start
  49.4 2.9 collective-permute-start.1
  52.3 66.0 %collective-permute-done = bf16[3,256,1,2048]{3,1,0,2:T(8,128)(2,1)S(1)} collective-permute-done((bf16[3,256,1,2048]{3,1,0,2:T(8,128)(2,1)S(1)}, bf16[3,256,1,2048]{3,1,0,2:T(8,128)(2,1)S(1)}, u32[]{:S(2)}, u32[]{:S(2)}) %collective-permute-start) | collective-permute-done | bytes 3145760 | tf_op jit(solution)/shard_map/ppermute | solution.py:38
  118.3 0.5 collective-permute-start.2
  118.8 0.9 collective-permute-done.1
  119.7 0.2 copy-done
  120.0 3.0 collective-permute-start.3
  122.9 64.1 %collective-permute-done.2 = bf16[3,256,1,2048]{3,1,0,2:T(8,128)(2,1)} collective-permute-done((bf16[3,256,1,2048]{3,1,0,2:T(8,128)(2,1)S(1)}, bf16[3,256,1,2048]{3,1,0,2:T(8,128)(2,1)}, u32[]{:S(2)}, u32[]{:S(2)}) %collective-permute-start.2) | collective-permute-done | bytes 3145760 | tf_op jit(solution)/shard_map/ppermute | solution.py:38
  187.0 0.0 collective-permute-start.4
  187.0 17.4 %broadcast_in_dim.42 = bf16[3,256,8,2048]{3,0,2,1:T(4,128)(2,1)} broadcast(bf16[]{:T(256)} %constant.58.clone.1), dimensions={} | broadcast | bytes 25165826 | tf_op jit(solution)/shard_map/broadcast_in_dim | solution.py:32
  204.4 4.7 copy_dynamic-update-slice_fusion.7
  209.1 0.0 collective-permute-done.3
  209.1 2.6 collective-permute-start.5
  211.7 4.7 copy_dynamic-update-slice_fusion.6
  216.4 19.6 %collective-permute-done.4 = bf16[3,256,1,2048]{3,1,0,2:T(8,128)(2,1)} collective-permute-done((bf16[3,256,1,2048]{3,1,0,2:T(8,128)(2,1)}, bf16[3,256,1,2048]{3,1,0,2:T(8,128)(2,1)}, u32[]{:S(2)}, u32[]{:S(2)}) %collective-permute-start.4) | collective-permute-done | bytes 3145760 | tf_op jit(solution)/shard_map/ppermute | solution.py:38
  236.1 0.2 collective-permute-start.6
  236.2 6.6 copy_dynamic-update-slice_fusion.5
  242.8 6.5 copy_dynamic-update-slice_fusion.4
  249.3 6.5 copy_dynamic-update-slice_fusion.3
  255.8 6.5 copy_dynamic-update-slice_fusion.2
  262.4 14.7 %collective-permute-done.5 = bf16[3,256,1,2048]{3,1,0,2:T(8,128)(2,1)S(1)} collective-permute-done((bf16[3,256,1,2048]{3,1,0,2:T(8,128)(2,1)}, bf16[3,256,1,2048]{3,1,0,2:T(8,128)(2,1)S(1)}, u32[]{:S(2)}, u32[]{:S(2)}) %collective-permute-start.5) | collective-permute-done | bytes 3145760 | tf_op jit(solution)/shard_map/ppermute | solution.py:43
  277.1 4.8 copy_dynamic-update-slice_fusion.1
  281.9 10.3 %collective-permute-done.6 = bf16[3,256,1,2048]{3,1,0,2:T(8,128)(2,1)S(1)} collective-permute-done((bf16[3,256,1,2048]{3,1,0,2:T(8,128)(2,1)}, bf16[3,256,1,2048]{3,1,0,2:T(8,128)(2,1)S(1)}, u32[]{:S(2)}, u32[]{:S(2)}) %collective-permute-start.6) | collective-permute-done | bytes 3145760 | tf_op jit(solution)/shard_map/ppermute | solution.py:38
  292.2 4.6 copy_dynamic-update-slice_fusion
  296.9 30.6 %fusion.4 = bf16[4,256,8,2048]{3,0,2,1:T(4,128)(2,1)} fusion(bf16[3,256,8,2048]{3,0,2,1:T(4,128)(2,1)} %copy_dynamic-update-slice_fusion, s32[3]{0:T(128)S(1)} %fusion.8), kind=kOutput, calls=%fused_computation.25 | convolution fusion | flops 100663312 | bytes 58720268 | tf_op jit(solution)/shard_map/kt,kjrb->tjrb/dot_general | solution.py:50
  327.5 30.0 %copy.44 = bf16[4,256,8,2048]{3,2,1,0:T(8,128)(2,1)} copy(bf16[4,256,8,2048]{3,0,2,1:T(4,128)(2,1)} %fusion.4) | data formatting | bytes 67108864 | tf_op jit(solution)/shard_map/kt,kjrb->tjrb/dot_general | solution.py:50
  357.4 44.0 %fusion.9 = f32[2048,1024]{1,0:T(8,128)} fusion(bf16[8192,2048]{1,0:T(8,128)(2,1)} %bitcast.49, bf16[1024,8192]{0,1:T(8,128)(2,1)} %all-gather.2.cloned.1.call-done), kind=kOutput, calls=%fused_computation.29 | convolution fusion | flops 34359738368 | bytes 58720256 | tf_op jit(solution)/shard_map/dot_general | solution.py:51
  401.5 9.2 %copy.45 = f32[1024,256,8]{1,0,2:T(8,128)} copy(f32[1024,256,8]{0,2,1:T(8,128)} %bitcast.47) | data formatting | bytes 16777216 | tf_op jit(solution)/shard_map/reshape | solution.py:56
  410.7 101.6 %all_to_all.34 = f32[1024,256,8]{1,0,2:T(8,128)S(1)} all-to-all(f32[1024,256,8]{1,0,2:T(8,128)} %copy.45), channel_id=1, replica_groups=mesh['row'=8,'col'=4] {'row'}, dimensions={2} | all-to-all | bytes 16777216 | tf_op jit(solution)/shard_map/all_to_all | solution.py:57
  512.4 8.1 %copy.46 = f32[1024,256,8]{1,2,0:T(8,128)} copy(f32[1024,256,8]{1,0,2:T(8,128)S(1)} %all_to_all.34) | data formatting | bytes 16777216 | tf_op jit(solution)/shard_map/all_to_all | solution.py:57
  520.5 5.8 all-to-all-start.1
  526.2 0.0 copy-done.2
  526.3 0.3 reshape.52
  526.6 0.4 dynamic-slice_reduce_fusion
  527.0 0.5 select_reduce_fusion.1
  527.4 0.9 select_reduce_fusion
  528.4 180.7 %all-to-all-done.1 = f32[4,2048,256]{2,1,0:T(8,128)} async-done(((f32[4,2048,256]{2,1,0:T(8,128)}), f32[4,2048,256]{2,1,0:T(8,128)}, u32[]{:S(2)}, u32[]{:S(2)}) %all-to-all-start.1) | async-done | bytes 8388640 | tf_op jit(solution)/shard_map/all_to_all | solution.py:61
  709.0 4.4 copy.51
  713.5 9.6 %fusion.2 = f32[1024,1,2048]{0,2,1:T(8,128)} fusion(f32[2048,1024]{1,0:T(8,128)S(1)} %bitcast.48, f32[2048,1024]{1,0:T(8,128)} %fusion.9, f32[1024,1,2048]{0,2,1:T(8,128)} %copy.35, f32[2048]{0:T(1024)S(1)} %select_reduce_fusion, f32[1024]{0:T(1024)S(1)} %select_reduce_fusion.1), kind=kLoop, calls=%fused_computation.4 | loop fusion | flops 10485760 | bytes 33566720 | tf_op jit(solution)/shard_map/broadcast_in_dim | solution.py:71
  723.1 20.5 %copy.48 = f32[1024,1,2048]{2,1,0:T(1,128)} copy(f32[1024,1,2048]{0,2,1:T(8,128)} %fusion.2) | data formatting | bytes 16777216 | tf_op jit(solution)/shard_map/broadcast_in_dim | solution.py:71
  (12 shorter events, 0.0 us)
Async XLA Ops:
  6.5 350.9 %all-gather.2.cloned.1.call-start = ((), (), s32[]{:S(2)}) async-start(), calls=%async_computation.2 | async-start | bytes 20971520 | tf_op jit(solution)/shard_map/all_gather | solution.py:52
  40.3 4.8 copy-start.4
  48.9 69.5 %collective-permute-start = (bf16[3,256,1,2048]{3,1,0,2:T(8,128)(2,1)S(1)}, bf16[3,256,1,2048]{3,1,0,2:T(8,128)(2,1)S(1)}, u32[]{:S(2)}, u32[]{:S(2)}) collective-permute-start(bf16[3,256,1,2048]{3,1,0,2:T(8,128)(2,1)S(1)} %bitcast.52), channel_id=1, source_target_pairs={{0,4},{4,8},{8,12},{12,16},{16,20},{20,24},{24,28},{28,0},{1,5},{5... | collective-permute-start | bytes 9437192 | tf_op jit(solution)/shard_map/ppermute | solution.py:38
  49.4 70.3 %collective-permute-start.1 = (bf16[3,256,1,2048]{3,1,0,2:T(8,128)(2,1)S(1)}, bf16[3,256,1,2048]{3,1,0,2:T(8,128)(2,1)}, u32[]{:S(2)}, u32[]{:S(2)}) collective-permute-start(bf16[3,256,1,2048]{3,1,0,2:T(8,128)(2,1)S(1)} %bitcast.53), channel_id=1, source_target_pairs={{0,28},{4,0},{8,4},{12,8},{16,12},{20,16},{24,20},{28,24},{1,29},{... | collective-permute-start | bytes 9437192 | tf_op jit(solution)/shard_map/ppermute | solution.py:43
  118.3 1.6 copy-start
  118.3 68.7 %collective-permute-start.2 = (bf16[3,256,1,2048]{3,1,0,2:T(8,128)(2,1)S(1)}, bf16[3,256,1,2048]{3,1,0,2:T(8,128)(2,1)}, u32[]{:S(2)}, u32[]{:S(2)}) collective-permute-start(bf16[3,256,1,2048]{3,1,0,2:T(8,128)(2,1)S(1)} %collective-permute-done), channel_id=1, source_target_pairs={{0,4},{4,8},{8,12},{12,16},{16,20},{20,24},{24,28},{28,0},{1,5},{5... | collective-permute-start | bytes 9437192 | tf_op jit(solution)/shard_map/ppermute | solution.py:38
  120.0 89.2 %collective-permute-start.3 = (bf16[3,256,1,2048]{3,1,0,2:T(8,128)(2,1)}, bf16[3,256,1,2048]{3,1,0,2:T(8,128)(2,1)}, u32[]{:S(2)}, u32[]{:S(2)}) collective-permute-start(bf16[3,256,1,2048]{3,1,0,2:T(8,128)(2,1)} %collective-permute-done.1), channel_id=1, source_target_pairs={{0,28},{4,0},{8,4},{12,8},{16,12},{20,16},{24,20},{28,24},{1,29},{... | collective-permute-start | bytes 9437192 | tf_op jit(solution)/shard_map/ppermute | solution.py:43
  187.0 49.0 %collective-permute-start.4 = (bf16[3,256,1,2048]{3,1,0,2:T(8,128)(2,1)}, bf16[3,256,1,2048]{3,1,0,2:T(8,128)(2,1)}, u32[]{:S(2)}, u32[]{:S(2)}) collective-permute-start(bf16[3,256,1,2048]{3,1,0,2:T(8,128)(2,1)} %collective-permute-done.2), channel_id=1, source_target_pairs={{0,4},{4,8},{8,12},{12,16},{16,20},{20,24},{24,28},{28,0},{1,5},{5... | collective-permute-start | bytes 9437192 | tf_op jit(solution)/shard_map/ppermute | solution.py:38
  204.4 7.3 copy-start.1
  209.1 68.0 %collective-permute-start.5 = (bf16[3,256,1,2048]{3,1,0,2:T(8,128)(2,1)}, bf16[3,256,1,2048]{3,1,0,2:T(8,128)(2,1)S(1)}, u32[]{:S(2)}, u32[]{:S(2)}) collective-permute-start(bf16[3,256,1,2048]{3,1,0,2:T(8,128)(2,1)} %collective-permute-done.3), channel_id=1, source_target_pairs={{0,28},{4,0},{8,4},{12,8},{16,12},{20,16},{24,20},{28,24},{1,29},{... | collective-permute-start | bytes 9437192 | tf_op jit(solution)/shard_map/ppermute | solution.py:43
  236.1 56.2 %collective-permute-start.6 = (bf16[3,256,1,2048]{3,1,0,2:T(8,128)(2,1)}, bf16[3,256,1,2048]{3,1,0,2:T(8,128)(2,1)S(1)}, u32[]{:S(2)}, u32[]{:S(2)}) collective-permute-start(bf16[3,256,1,2048]{3,1,0,2:T(8,128)(2,1)} %collective-permute-done.4), channel_id=1, source_target_pairs={{0,4},{4,8},{8,12},{12,16},{16,20},{20,24},{24,28},{28,0},{1,5},{5... | collective-permute-start | bytes 9437192 | tf_op jit(solution)/shard_map/ppermute | solution.py:38
  520.5 5.8 copy-start.2
  520.5 6.5 copy-start.3
  520.5 188.6 %all-to-all-start.1 = ((f32[4,2048,256]{2,1,0:T(8,128)}), f32[4,2048,256]{2,1,0:T(8,128)}, u32[]{:S(2)}, u32[]{:S(2)}) async-start(f32[4,2048,256]{2,1,0:T(8,128)} %bitcast.50), calls=%async_computation.1 | async-start | bytes 16777216 | tf_op jit(solution)/shard_map/all_to_all | solution.py:61
Sparse Core Ops, SparseCore 0:
  33.3 289.4 all-gather.1
